TPU v7x, 32 devices: a whole 2x2x4 slice. The times are simulated.
32 devices in a mesh: site: 4 (over y, x), sector: 8 (over z, core).
Axes of the slice: x: 2, y: 2, z: 4, core: 2. Of those that a mesh axis runs over, the one named last changes fastest.
Arguments:
- boundary: bfloat16 [4, 2048, 32, 256], P('site', 'sector'), may hold values from -0.375 to 0.375
- peps_row: bfloat16 [4, 32, 8], P('site'), may hold values from -1 to 1
- sketch: bfloat16 [4, 2048, 8, 256], P('site', 'sector'), may hold values from -0.125 to 0.125
- charges: int32 [4, 8], P('site'), may hold values from -1 to 1
- left_edge: bfloat16 [512, 2048], P(None, 'sector'), may hold values from -6 to 6
Outputs:
- environments: float32 [4, 512, 2048], P('site', None, 'sector')
Inputs may be any that keep to these rules, and one draw needn't show every extreme that they name: `charges`: each entry is a charge change of -1, 0 or +1.
All inputs are finite; a program needn't handle non-finite values.
Results may differ from a plain program's by a relative error of at most 0.0003.
Values sent between devices are 32-bit elements; how exact they have to be, the bound alone decides.
A program may use at most 64 MiB of HBM per device.

v0:
```python
import jax
import jax.numpy as jnp
from jax import lax
from jax.sharding import PartitionSpec as P


def with_halo(block, sides, width):
    for axis, dim in sides:
        count = lax.axis_size(axis)
        forward = [(i, i + 1) for i in range(count - 1)]
        backward = [(target, source) for source, target in forward]
        low = lax.ppermute(
            lax.slice_in_dim(block, block.shape[dim] - width, None, axis=dim), axis, forward
        )
        high = lax.ppermute(lax.slice_in_dim(block, 0, width, axis=dim), axis, backward)
        block = jnp.concatenate([low, block, high], axis=dim)
    return block


def local(boundary, peps_row, sketch, charges, left_edge):
    total_rows = left_edge.shape[0]
    absorbed = jnp.einsum("jwpv,jpl->jwlv", boundary, peps_row, preferred_element_type=jnp.float32)
    sketch_wide = sketch.astype(jnp.float32)
    onehot = (charges[:, :, None] == jnp.arange(-1, 2, dtype=jnp.int32)[None, None, :]).astype(
        jnp.float32
    )
    site_devices = lax.axis_size("site")
    position = lax.axis_index("site")
    own_maps = jnp.einsum(
        "jwlv,jvlu,jls->jswu", absorbed, sketch_wide, onehot, precision=lax.Precision.HIGHEST
    )
    all_maps = lax.all_gather(own_maps, "site", axis=0, tiled=True)
    share_rows = total_rows // site_devices
    start_state = lax.dynamic_slice_in_dim(left_edge, position * share_rows, share_rows, 0).astype(
        jnp.float32
    )

    def row_site(state_rows, site_map):
        parts = jnp.einsum("rw,swu->sru", state_rows, site_map, precision=lax.Precision.HIGHEST)
        outflow = jnp.stack([parts[0], parts[2]], axis=0)
        padded = with_halo(outflow, (("sector", 0),), 1)
        updated = parts[1] + padded[0] + padded[3]
        return (updated, updated)

    final_rows, stacked = lax.scan(row_site, start_state, all_maps)
    return lax.all_to_all(stacked, "site", split_axis=0, concat_axis=1, tiled=True)


def solution(mesh):
    in_specs = (
        P("site", "sector", None, None),
        P("site", None, None),
        P("site", "sector", None, None),
        P("site", None),
        P(None, "sector"),
    )
    out_specs = P("site", None, "sector")
    return jax.shard_map(local, mesh=mesh, in_specs=in_specs, out_specs=out_specs, check_vma=False)
```

profile of v0, /device:TPU:8, one launch (start us, length us, event | category | flops | bytes accessed | tf_op | source)
XLA Modules:
  0.0 126.1 jit_solution(7024198187606349648)
XLA Ops:
  6.5 2.9 %fusion.12 = f32[256,8,256]{2,1,0:T(8,128)S(1)} fusion(bf16[1,256,32,256]{3,2,1,0:T(8,128)(2,1)} %param.7, bf16[1,32,8]{1,2,0:T(8,128)(2,1)} %param.8), kind=kOutput, calls=%fused_computation.15 | convolution fusion | flops 33554432 | bytes 6291968 | tf_op jit(solution)/shard_map/jwpv,jpl->jwlv/dot_general | solution.py:22
  9.5 3.1 %fusion.10 = f32[8,256,256]{2,1,0:T(8,128)} fusion(f32[256,8,256]{2,1,0:T(8,128)S(1)} %fusion.12, bf16[256,8,256]{2,1,0:T(8,128)(2,1)S(1)} %bitcast.47), kind=kOutput, calls=%fused_computation.13 | convolution fusion | flops 1610612736 | bytes 5242880 | tf_op jit(solution)/shard_map/jwlv,jvlu,jls->jswu/dot_general | solution.py:29
  12.6 2.2 %copy.18 = f32[8,256,256]{1,0,2:T(8,128)S(1)} copy(f32[8,256,256]{2,1,0:T(8,128)} %fusion.10) | data formatting | bytes 4194304 | tf_op jit(solution)/shard_map/jwlv,jvlu,jls->jswu/dot_general | solution.py:29
  14.8 2.1 %fusion.15 = f32[1,3,256,256]{2,1,3,0:T(4,128)} fusion(f32[8,256,256]{1,0,2:T(8,128)S(1)} %copy.18, s32[8]{0:T(128)S(1)} %bitcast.48, s32[3]{0:T(128)S(1)} %iota_add_fusion), kind=kOutput, calls=%fused_computation.16 | convolution fusion | flops 18874392 | bytes 2883628 | tf_op jit(solution)/shard_map/jwlv,jvlu,jls->jswu/dot_general | solution.py:29
  16.9 2.4 %copy.12 = f32[1,3,256,256]{3,2,1,0:T(8,128)} copy(f32[1,3,256,256]{2,1,3,0:T(4,128)} %fusion.15) | data formatting | bytes 1572864 | tf_op jit(solution)/shard_map/jwlv,jvlu,jls->jswu/transpose | solution.py:29
  20.3 44.2 %all-gather.2.cloned.1.call-done = f32[4,3,256,256]{3,2,1,0:T(8,128)} async-done(((f32[1,3,256,256]{3,2,1,0:T(8,128)}), f32[4,3,256,256]{3,2,1,0:T(8,128)}) %all-gather.2.cloned.1.call-update) | async-done | bytes 3145744 | tf_op jit(solution)/shard_map/all_gather | solution.py:32
  64.5 43.3 %while.12 = (s32[]{:T(128)}, f32[128,256]{0,1:T(8,128)S(1)}, f32[4,128,256]{1,2,0:T(8,128)S(1)}, f32[4,3,256,256]{3,2,1,0:T(8,128)}, s32[]{:T(128)}) while((s32[]{:T(128)}, f32[128,256]{0,1:T(8,128)S(1)}, f32[4,128,256]{1,2,0:T(8,128)S(1)}, f32[4,3,256,256]{3,2,1,0:T(8,128)}, s32[]{:T(128)}) %tuple.26), condition=%wide.region_1.2_spmd, body=%wide.region_0.1_spmd.sunk | while | flops 302055424 | bytes 3539101 | solution.py:45
  64.5 2.5 %convolution_bitcast_fusion.2 = f32[3,128,256]{1,2,0:T(8,128)S(1)} fusion(f32[4,3,256,256]{3,2,1,0:T(8,128)} %get-tuple-element.94, s32[]{:T(128)S(6)} %copy.30, f32[128,256]{0,1:T(8,128)S(1)} %get-tuple-element.87), kind=kOutput, calls=%fused_computation.clone.1 | convolution fusion | flops 301989888 | bytes 1310724 | tf_op jit(solution)/shard_map/while/body/eval_jaxpr/rw,swu->sru/dot_general | solution.py:39
  67.0 1.9 %collective-permute-start = (f32[1,128,256]{1,2,0:T(8,128)S(1)}, f32[1,128,256]{1,2,0:T(8,128)S(1)}, u32[]{:S(2)}, u32[]{:S(2)}) collective-permute-start(f32[1,128,256]{1,2,0:T(8,128)S(1)} %get-tuple-element.77), channel_id=1, source_target_pairs={{1,0},{2,1},{3,2},{4,3},{5,4},{6,5},{7,6},{9,8},{10,9},{11,10},{12... | collective-permute-start | bytes 393224 | tf_op jit(solution)/shard_map/while/body/eval_jaxpr/ppermute | solution.py:15
  69.0 2.4 %collective-permute-start.1 = (f32[1,128,256]{1,2,0:T(8,128)S(1)}, f32[1,128,256]{1,2,0:T(8,128)S(1)}, u32[]{:S(2)}, u32[]{:S(2)}) collective-permute-start(f32[1,128,256]{1,2,0:T(8,128)S(1)} %get-tuple-element.78), channel_id=1, source_target_pairs={{0,1},{1,2},{2,3},{3,4},{4,5},{5,6},{6,7},{8,9},{9,10},{10,11},{11... | collective-permute-start | bytes 393224 | tf_op jit(solution)/shard_map/while/body/eval_jaxpr/ppermute | solution.py:12
  71.5 3.8 %collective-permute-done.1 = f32[1,128,256]{1,2,0:T(8,128)S(1)} collective-permute-done((f32[1,128,256]{1,2,0:T(8,128)S(1)}, f32[1,128,256]{1,2,0:T(8,128)S(1)}, u32[]{:S(2)}, u32[]{:S(2)}) %collective-permute-start.1) | collective-permute-done | bytes 131104 | tf_op jit(solution)/shard_map/while/body/eval_jaxpr/ppermute | solution.py:12
  75.3 2.5 %convolution_bitcast_fusion.2 = f32[3,128,256]{1,2,0:T(8,128)S(1)} fusion(f32[4,3,256,256]{3,2,1,0:T(8,128)} %get-tuple-element.94, s32[]{:T(128)S(6)} %copy.30, f32[128,256]{0,1:T(8,128)S(1)} %get-tuple-element.87), kind=kOutput, calls=%fused_computation.clone.1 | convolution fusion | flops 301989888 | bytes 1310724 | tf_op jit(solution)/shard_map/while/body/eval_jaxpr/rw,swu->sru/dot_general | solution.py:39
  77.9 1.9 %collective-permute-start = (f32[1,128,256]{1,2,0:T(8,128)S(1)}, f32[1,128,256]{1,2,0:T(8,128)S(1)}, u32[]{:S(2)}, u32[]{:S(2)}) collective-permute-start(f32[1,128,256]{1,2,0:T(8,128)S(1)} %get-tuple-element.77), channel_id=1, source_target_pairs={{1,0},{2,1},{3,2},{4,3},{5,4},{6,5},{7,6},{9,8},{10,9},{11,10},{12... | collective-permute-start | bytes 393224 | tf_op jit(solution)/shard_map/while/body/eval_jaxpr/ppermute | solution.py:15
  79.8 2.4 %collective-permute-start.1 = (f32[1,128,256]{1,2,0:T(8,128)S(1)}, f32[1,128,256]{1,2,0:T(8,128)S(1)}, u32[]{:S(2)}, u32[]{:S(2)}) collective-permute-start(f32[1,128,256]{1,2,0:T(8,128)S(1)} %get-tuple-element.78), channel_id=1, source_target_pairs={{0,1},{1,2},{2,3},{3,4},{4,5},{5,6},{6,7},{8,9},{9,10},{10,11},{11... | collective-permute-start | bytes 393224 | tf_op jit(solution)/shard_map/while/body/eval_jaxpr/ppermute | solution.py:12
  82.3 3.8 %collective-permute-done.1 = f32[1,128,256]{1,2,0:T(8,128)S(1)} collective-permute-done((f32[1,128,256]{1,2,0:T(8,128)S(1)}, f32[1,128,256]{1,2,0:T(8,128)S(1)}, u32[]{:S(2)}, u32[]{:S(2)}) %collective-permute-start.1) | collective-permute-done | bytes 131104 | tf_op jit(solution)/shard_map/while/body/eval_jaxpr/ppermute | solution.py:12
  86.1 2.5 %convolution_bitcast_fusion.2 = f32[3,128,256]{1,2,0:T(8,128)S(1)} fusion(f32[4,3,256,256]{3,2,1,0:T(8,128)} %get-tuple-element.94, s32[]{:T(128)S(6)} %copy.30, f32[128,256]{0,1:T(8,128)S(1)} %get-tuple-element.87), kind=kOutput, calls=%fused_computation.clone.1 | convolution fusion | flops 301989888 | bytes 1310724 | tf_op jit(solution)/shard_map/while/body/eval_jaxpr/rw,swu->sru/dot_general | solution.py:39
  88.7 1.9 %collective-permute-start = (f32[1,128,256]{1,2,0:T(8,128)S(1)}, f32[1,128,256]{1,2,0:T(8,128)S(1)}, u32[]{:S(2)}, u32[]{:S(2)}) collective-permute-start(f32[1,128,256]{1,2,0:T(8,128)S(1)} %get-tuple-element.77), channel_id=1, source_target_pairs={{1,0},{2,1},{3,2},{4,3},{5,4},{6,5},{7,6},{9,8},{10,9},{11,10},{12... | collective-permute-start | bytes 393224 | tf_op jit(solution)/shard_map/while/body/eval_jaxpr/ppermute | solution.py:15
  90.6 2.4 %collective-permute-start.1 = (f32[1,128,256]{1,2,0:T(8,128)S(1)}, f32[1,128,256]{1,2,0:T(8,128)S(1)}, u32[]{:S(2)}, u32[]{:S(2)}) collective-permute-start(f32[1,128,256]{1,2,0:T(8,128)S(1)} %get-tuple-element.78), channel_id=1, source_target_pairs={{0,1},{1,2},{2,3},{3,4},{4,5},{5,6},{6,7},{8,9},{9,10},{10,11},{11... | collective-permute-start | bytes 393224 | tf_op jit(solution)/shard_map/while/body/eval_jaxpr/ppermute | solution.py:12
  93.1 3.8 %collective-permute-done.1 = f32[1,128,256]{1,2,0:T(8,128)S(1)} collective-permute-done((f32[1,128,256]{1,2,0:T(8,128)S(1)}, f32[1,128,256]{1,2,0:T(8,128)S(1)}, u32[]{:S(2)}, u32[]{:S(2)}) %collective-permute-start.1) | collective-permute-done | bytes 131104 | tf_op jit(solution)/shard_map/while/body/eval_jaxpr/ppermute | solution.py:12
  96.9 2.5 %convolution_bitcast_fusion.2 = f32[3,128,256]{1,2,0:T(8,128)S(1)} fusion(f32[4,3,256,256]{3,2,1,0:T(8,128)} %get-tuple-element.94, s32[]{:T(128)S(6)} %copy.30, f32[128,256]{0,1:T(8,128)S(1)} %get-tuple-element.87), kind=kOutput, calls=%fused_computation.clone.1 | convolution fusion | flops 301989888 | bytes 1310724 | tf_op jit(solution)/shard_map/while/body/eval_jaxpr/rw,swu->sru/dot_general | solution.py:39
  99.5 1.9 %collective-permute-start = (f32[1,128,256]{1,2,0:T(8,128)S(1)}, f32[1,128,256]{1,2,0:T(8,128)S(1)}, u32[]{:S(2)}, u32[]{:S(2)}) collective-permute-start(f32[1,128,256]{1,2,0:T(8,128)S(1)} %get-tuple-element.77), channel_id=1, source_target_pairs={{1,0},{2,1},{3,2},{4,3},{5,4},{6,5},{7,6},{9,8},{10,9},{11,10},{12... | collective-permute-start | bytes 393224 | tf_op jit(solution)/shard_map/while/body/eval_jaxpr/ppermute | solution.py:15
  101.4 2.4 %collective-permute-start.1 = (f32[1,128,256]{1,2,0:T(8,128)S(1)}, f32[1,128,256]{1,2,0:T(8,128)S(1)}, u32[]{:S(2)}, u32[]{:S(2)}) collective-permute-start(f32[1,128,256]{1,2,0:T(8,128)S(1)} %get-tuple-element.78), channel_id=1, source_target_pairs={{0,1},{1,2},{2,3},{3,4},{4,5},{5,6},{6,7},{8,9},{9,10},{10,11},{11... | collective-permute-start | bytes 393224 | tf_op jit(solution)/shard_map/while/body/eval_jaxpr/ppermute | solution.py:12
  103.9 3.8 %collective-permute-done.1 = f32[1,128,256]{1,2,0:T(8,128)S(1)} collective-permute-done((f32[1,128,256]{1,2,0:T(8,128)S(1)}, f32[1,128,256]{1,2,0:T(8,128)S(1)}, u32[]{:S(2)}, u32[]{:S(2)}) %collective-permute-start.1) | collective-permute-done | bytes 131104 | tf_op jit(solution)/shard_map/while/body/eval_jaxpr/ppermute | solution.py:12
  107.8 10.5 %all_to_all.12 = f32[4,128,256]{1,2,0:T(8,128)S(1)} all-to-all(f32[4,128,256]{1,2,0:T(8,128)S(1)} %get-tuple-element.27), channel_id=1, replica_groups=mesh['site'=4,'sector'=8] {'site'}, dimensions={0} | all-to-all | bytes 1048576 | tf_op jit(solution)/shard_map/all_to_all | solution.py:46
  (24 shorter events, 2.5 us)
Async XLA Ops:
  6.5 3.0 %copy-start = (bf16[1,256,8,256]{3,2,1,0:T(8,128)(2,1)S(1)}, bf16[1,256,8,256]{3,2,1,0:T(8,128)(2,1)}, u32[]{:S(2)}) copy-start(bf16[1,256,8,256]{3,2,1,0:T(8,128)(2,1)} %param.9) | copy-start | bytes 3145732
  6.5 57.9 %all-gather.2.cloned.1.call-start = ((), (), s32[]{:S(2)}) async-start(), calls=%async_computation.1 | async-start | bytes 3932160 | tf_op jit(solution)/shard_map/all_gather | solution.py:32
  12.6 2.2 %copy-start.1 = (s32[1,8]{1,0:T(1,128)S(1)}, s32[1,8]{1,0:T(1,128)}, u32[]{:S(2)}) copy-start(s32[1,8]{1,0:T(1,128)} %param.10) | copy-start | bytes 100
  67.0 4.4 %collective-permute-start = (f32[1,128,256]{1,2,0:T(8,128)S(1)}, f32[1,128,256]{1,2,0:T(8,128)S(1)}, u32[]{:S(2)}, u32[]{:S(2)}) collective-permute-start(f32[1,128,256]{1,2,0:T(8,128)S(1)} %get-tuple-element.77), channel_id=1, source_target_pairs={{1,0},{2,1},{3,2},{4,3},{5,4},{6,5},{7,6},{9,8},{10,9},{11,10},{12... | collective-permute-start | bytes 393224 | tf_op jit(solution)/shard_map/while/body/eval_jaxpr/ppermute | solution.py:15
  69.0 6.3 %collective-permute-start.1 = (f32[1,128,256]{1,2,0:T(8,128)S(1)}, f32[1,128,256]{1,2,0:T(8,128)S(1)}, u32[]{:S(2)}, u32[]{:S(2)}) collective-permute-start(f32[1,128,256]{1,2,0:T(8,128)S(1)} %get-tuple-element.78), channel_id=1, source_target_pairs={{0,1},{1,2},{2,3},{3,4},{4,5},{5,6},{6,7},{8,9},{9,10},{10,11},{11... | collective-permute-start | bytes 393224 | tf_op jit(solution)/shard_map/while/body/eval_jaxpr/ppermute | solution.py:12
  77.9 4.4 %collective-permute-start = (f32[1,128,256]{1,2,0:T(8,128)S(1)}, f32[1,128,256]{1,2,0:T(8,128)S(1)}, u32[]{:S(2)}, u32[]{:S(2)}) collective-permute-start(f32[1,128,256]{1,2,0:T(8,128)S(1)} %get-tuple-element.77), channel_id=1, source_target_pairs={{1,0},{2,1},{3,2},{4,3},{5,4},{6,5},{7,6},{9,8},{10,9},{11,10},{12... | collective-permute-start | bytes 393224 | tf_op jit(solution)/shard_map/while/body/eval_jaxpr/ppermute | solution.py:15
  79.8 6.3 %collective-permute-start.1 = (f32[1,128,256]{1,2,0:T(8,128)S(1)}, f32[1,128,256]{1,2,0:T(8,128)S(1)}, u32[]{:S(2)}, u32[]{:S(2)}) collective-permute-start(f32[1,128,256]{1,2,0:T(8,128)S(1)} %get-tuple-element.78), channel_id=1, source_target_pairs={{0,1},{1,2},{2,3},{3,4},{4,5},{5,6},{6,7},{8,9},{9,10},{10,11},{11... | collective-permute-start | bytes 393224 | tf_op jit(solution)/shard_map/while/body/eval_jaxpr/ppermute | solution.py:12
  88.7 4.4 %collective-permute-start = (f32[1,128,256]{1,2,0:T(8,128)S(1)}, f32[1,128,256]{1,2,0:T(8,128)S(1)}, u32[]{:S(2)}, u32[]{:S(2)}) collective-permute-start(f32[1,128,256]{1,2,0:T(8,128)S(1)} %get-tuple-element.77), channel_id=1, source_target_pairs={{1,0},{2,1},{3,2},{4,3},{5,4},{6,5},{7,6},{9,8},{10,9},{11,10},{12... | collective-permute-start | bytes 393224 | tf_op jit(solution)/shard_map/while/body/eval_jaxpr/ppermute | solution.py:15
  90.6 6.3 %collective-permute-start.1 = (f32[1,128,256]{1,2,0:T(8,128)S(1)}, f32[1,128,256]{1,2,0:T(8,128)S(1)}, u32[]{:S(2)}, u32[]{:S(2)}) collective-permute-start(f32[1,128,256]{1,2,0:T(8,128)S(1)} %get-tuple-element.78), channel_id=1, source_target_pairs={{0,1},{1,2},{2,3},{3,4},{4,5},{5,6},{6,7},{8,9},{9,10},{10,11},{11... | collective-permute-start | bytes 393224 | tf_op jit(solution)/shard_map/while/body/eval_jaxpr/ppermute | solution.py:12
  99.5 4.4 %collective-permute-start = (f32[1,128,256]{1,2,0:T(8,128)S(1)}, f32[1,128,256]{1,2,0:T(8,128)S(1)}, u32[]{:S(2)}, u32[]{:S(2)}) collective-permute-start(f32[1,128,256]{1,2,0:T(8,128)S(1)} %get-tuple-element.77), channel_id=1, source_target_pairs={{1,0},{2,1},{3,2},{4,3},{5,4},{6,5},{7,6},{9,8},{10,9},{11,10},{12... | collective-permute-start | bytes 393224 | tf_op jit(solution)/shard_map/while/body/eval_jaxpr/ppermute | solution.py:15
  101.4 6.3 %collective-permute-start.1 = (f32[1,128,256]{1,2,0:T(8,128)S(1)}, f32[1,128,256]{1,2,0:T(8,128)S(1)}, u32[]{:S(2)}, u32[]{:S(2)}) collective-permute-start(f32[1,128,256]{1,2,0:T(8,128)S(1)} %get-tuple-element.78), channel_id=1, source_target_pairs={{0,1},{1,2},{2,3},{3,4},{4,5},{5,6},{6,7},{8,9},{9,10},{10,11},{11... | collective-permute-start | bytes 393224 | tf_op jit(solution)/shard_map/while/body/eval_jaxpr/ppermute | solution.py:12
Sparse Core Ops, SparseCore 0:
  19.4 44.9 all-gather.1
where the time goes:
time: 127 us; the launch traced here: 126 us
  waiting for transfers between devices  59.7 us (47%)
  matrix products  18.2 us (14%)
  starting transfers between devices  17.3 us (14%)
  between operations  13.5 us (11%)
  blocking collectives  10.5 us (8%)
  local copies, waits for them, and re-layouts  6.64 us (5%)
    all_gather x1, waiting for transfers between devices, local(): all_maps = lax.all_gather(own_maps, 'site', axis=0, tiled=True)  44.2 us
    ppermute x4, waiting for transfers between devices, with_halo(): lax.ppermute(lax.slice_in_dim(block, block.shape[dim] - width, None, axis...  15.1 us
    all_to_all x1, blocking collectives, local(): lax.all_to_all(stacked, 'site', split_axis=0, concat_axis=1, tiled=True)  10.5 us
    dot_general x4, matrix products, row_site(): jnp.einsum('rw,swu->sru', state_rows, site_map, precision=lax.Precision.H...  10.1 us
    ppermute x4, starting transfers between devices, with_halo(): lax.ppermute(lax.slice_in_dim(block, block.shape[dim] - width, None, axis...  9.63 us
    ppermute x4, starting transfers between devices, with_halo(): lax.ppermute(lax.slice_in_dim(block, 0, width, axis=dim), axis, backward)  7.68 us
    dot_general x2, matrix products, local(): jnp.einsum('jwlv,jvlu,jls->jswu', absorbed, sketch_wide, onehot, precisio...  5.17 us
    dot_general x1, matrix products, local(): jnp.einsum('jwpv,jpl->jwlv', boundary, peps_row, preferred_element_type=j...  2.94 us
  transfers between devices with their start and end apart: 9, of which 9 were waited for; matrix products, arithmetic and copies ran while one was open for 1% of the time, Pallas kernels for 0%

commit v1 on v0

--- a/solution.py
+++ b/solution.py
@@ -2,6 +2,16 @@
 import jax.numpy as jnp
 from jax import lax
 from jax.sharding import PartitionSpec as P
+
+
+def pass_along(shard, name, dim):
+    n_dev = lax.axis_size(name)
+    held, blocks = (shard, [shard])
+    for _ in range(n_dev - 1):
+        held = lax.ppermute(held, name, [(i, (i + 1) % n_dev) for i in range(n_dev)])
+        blocks.insert(0, held)
+    flat = jnp.concatenate(blocks, axis=dim)
+    return jnp.roll(flat, (lax.axis_index(name) + 1) * shard.shape[dim], axis=dim)
 
 
 def with_halo(block, sides, width):
@@ -29,7 +39,7 @@
     own_maps = jnp.einsum(
         "jwlv,jvlu,jls->jswu", absorbed, sketch_wide, onehot, precision=lax.Precision.HIGHEST
     )
-    all_maps = lax.all_gather(own_maps, "site", axis=0, tiled=True)
+    all_maps = pass_along(own_maps, "site", 0)
     share_rows = total_rows // site_devices
     start_state = lax.dynamic_slice_in_dim(left_edge, position * share_rows, share_rows, 0).astype(
         jnp.float32

time: 127 us -> 132 us (1.039)
  between operations: 13.5 us -> 0.16 us
  local copies, waits for them, and re-layouts: 6.64 us -> 19.2 us
  waiting for transfers between devices: 59.7 us -> 66.8 us
  matrix products: 18.2 us -> 15 us
  starting transfers between devices: 17.3 us -> 19.4 us
    ppermute x0 -> x3, waiting for transfers between devices: none -> 51.3 us  [pass_along(): lax.ppermute(held, name, [(i, (i + 1) % n_dev) for i in range(n_dev)])]
    all_gather x1 -> x0, waiting for transfers between devices: 44.2 us -> none  [local(): all_maps = lax.all_gather(own_maps, 'site', axis=0, tiled=True)]
    ppermute x0 -> x3, local copies, waits for them, and re-layouts: none -> 6.44 us  [pass_along(): lax.ppermute(held, name, [(i, (i + 1) % n_dev) for i in range(n_dev)])]
    unnamed x5 -> x20, local copies, waits for them, and re-layouts: 0.12 us -> 5.3 us
    dot_general x4, matrix products: 10.1 us -> 7.66 us  [row_site(): jnp.einsum('rw,swu->sru', state_rows, site_map, precision=lax.Precision.H...]
    while x0 -> x1, local copies, waits for them, and re-layouts: none -> 2.19 us  [local(): final_rows, stacked = lax.scan(row_site, start_state, all_maps)]
    ppermute x0 -> x3, starting transfers between devices: none -> 2.14 us  [pass_along(): lax.ppermute(held, name, [(i, (i + 1) % n_dev) for i in range(n_dev)])]
    transpose x1, local copies, waits for them, and re-layouts: 2.38 us -> 0.32 us  [local(): jnp.einsum('jwlv,jvlu,jls->jswu', absorbed, sketch_wide, onehot, precisio...]
  transfers between devices with their start and end apart: 9 -> 11, of which waited for: 9 -> 11; matrix products, arithmetic and copies ran while one was open for 1% -> 4% of each run, Pallas kernels for 0% -> 0%
where the time goes in v1:
time: 132 us
  waiting for transfers between devices  66.8 us (51%)
  starting transfers between devices  19.4 us (15%)
  local copies, waits for them, and re-layouts  19.2 us (15%)
  matrix products  15 us (11%)
  blocking collectives  10.6 us (8%)
    ppermute x3, waiting for transfers between devices, pass_along(): lax.ppermute(held, name, [(i, (i + 1) % n_dev) for i in range(n_dev)])  51.3 us
    ppermute x4, waiting for transfers between devices, with_halo(): lax.ppermute(lax.slice_in_dim(block, block.shape[dim] - width, None, axis...  15.1 us
    all_to_all x1, blocking collectives, local(): lax.all_to_all(stacked, 'site', split_axis=0, concat_axis=1, tiled=True)  10.6 us
    ppermute x4, starting transfers between devices, with_halo(): lax.ppermute(lax.slice_in_dim(block, block.shape[dim] - width, None, axis...  9.63 us
    ppermute x4, starting transfers between devices, with_halo(): lax.ppermute(lax.slice_in_dim(block, 0, width, axis=dim), axis, backward)  7.68 us
    dot_general x4, matrix products, row_site(): jnp.einsum('rw,swu->sru', state_rows, site_map, precision=lax.Precision.H...  7.66 us
    ppermute x3, local copies, waits for them, and re-layouts, pass_along(): lax.ppermute(held, name, [(i, (i + 1) % n_dev) for i in range(n_dev)])  6.44 us
    unnamed x20, local copies, waits for them, and re-layouts  5.3 us
  transfers between devices with their start and end apart: 11, of which 11 were waited for; matrix products, arithmetic and copies ran while one was open for 4% of the time, Pallas kernels for 0%

profile of v1, /device:TPU:8, one launch (start us, length us, event | category | flops | bytes accessed | tf_op | source)
XLA Modules:
  0.0 131.5 jit_solution(14924236979588808242)
XLA Ops:
  0.0 2.9 %fusion.12 = f32[256,8,256]{2,1,0:T(8,128)S(1)} fusion(bf16[1,256,32,256]{3,2,1,0:T(8,128)(2,1)} %param.7, bf16[1,32,8]{1,2,0:T(8,128)(2,1)} %param.8), kind=kOutput, calls=%fused_computation.15 | convolution fusion | flops 33554432 | bytes 6291968 | tf_op jit(solution)/shard_map/jwpv,jpl->jwlv/dot_general | solution.py:32
  4.7 2.0 %copy.24 = f32[8,256,256]{1,0,2:T(8,128)} copy(f32[8,256,256]{2,1,0:T(8,128)S(1)} %fusion.10) | data formatting | bytes 4194304 | tf_op jit(solution)/shard_map/jwlv,jvlu,jls->jswu/dot_general | solution.py:39
  6.7 2.7 %fusion.15 = f32[1,3,256,256]{2,1,3,0:T(4,128)S(1)} fusion(f32[8,256,256]{1,0,2:T(8,128)} %copy.24, s32[8]{0:T(128)S(1)} %bitcast.47, s32[3]{0:T(128)S(1)} %iota_add_fusion), kind=kOutput, calls=%fused_computation.16 | convolution fusion | flops 18874392 | bytes 2883628 | tf_op jit(solution)/shard_map/jwlv,jvlu,jls->jswu/dot_general | solution.py:39
  11.3 18.7 %collective-permute-done.2 = f32[1,3,256,256]{3,2,1,0:T(8,128)S(1)} collective-permute-done((f32[1,3,256,256]{3,2,1,0:T(8,128)S(1)}, f32[1,3,256,256]{3,2,1,0:T(8,128)S(1)}, u32[]{:S(2)}, u32[]{:S(2)}) %collective-permute-start.2) | collective-permute-done | bytes 786464 | tf_op jit(solution)/shard_map/ppermute | solution.py:11
  31.5 18.8 %collective-permute-done.3 = f32[1,3,256,256]{3,2,1,0:T(8,128)} collective-permute-done((f32[1,3,256,256]{3,2,1,0:T(8,128)S(1)}, f32[1,3,256,256]{3,2,1,0:T(8,128)}, u32[]{:S(2)}, u32[]{:S(2)}) %collective-permute-start.3) | collective-permute-done | bytes 786464 | tf_op jit(solution)/shard_map/ppermute | solution.py:11
  52.8 2.4 %copy.14 = f32[1,3,256,256]{2,1,3,0:T(4,128)} copy(f32[1,3,256,256]{3,2,1,0:T(8,128)} %collective-permute-done.3) | data formatting | bytes 1572864 | tf_op jit(solution)/shard_map/ppermute | solution.py:11
  55.3 13.8 %collective-permute-done.4 = f32[1,3,256,256]{3,2,1,0:T(8,128)} collective-permute-done((f32[1,3,256,256]{3,2,1,0:T(8,128)}, f32[1,3,256,256]{3,2,1,0:T(8,128)}, u32[]{:S(2)}, u32[]{:S(2)}) %collective-permute-start.4) | collective-permute-done | bytes 786464 | tf_op jit(solution)/shard_map/ppermute | solution.py:11
  69.1 2.5 %copy.13 = f32[1,3,256,256]{2,1,3,0:T(4,128)} copy(f32[1,3,256,256]{3,2,1,0:T(8,128)} %collective-permute-done.4) | data formatting | bytes 1572864 | tf_op jit(solution)/shard_map/ppermute | solution.py:11
  76.9 2.2 %copy.19 = f32[4,3,256,256]{2,3,1,0:T(8,128)} copy(f32[4,3,256,256]{2,1,3,0:T(4,128)S(1)} %constant_dynamic-slice_fusion) | data formatting | bytes 6291456 | tf_op jit(solution)/shard_map/while | solution.py:55
  79.1 40.8 %while.12 = (s32[]{:T(128)}, f32[128,256]{0,1:T(8,128)S(1)}, f32[4,128,256]{1,2,0:T(8,128)S(1)}, f32[4,3,256,256]{2,3,1,0:T(8,128)}, s32[]{:T(128)}) while((s32[]{:T(128)}, f32[128,256]{0,1:T(8,128)S(1)}, f32[4,128,256]{1,2,0:T(8,128)S(1)}, f32[4,3,256,256]{2,3,1,0:T(8,128)}, s32[]{:T(128)}) %tuple.29), condition=%wide.region_1.2_spmd, body=%wide.region_0.1_spmd.sunk | while | flops 302055424 | bytes 3539101 | solution.py:55
  81.0 1.9 %collective-permute-start = (f32[1,128,256]{1,2,0:T(8,128)S(1)}, f32[1,128,256]{1,2,0:T(8,128)S(1)}, u32[]{:S(2)}, u32[]{:S(2)}) collective-permute-start(f32[1,128,256]{1,2,0:T(8,128)S(1)} %get-tuple-element.77), channel_id=1, source_target_pairs={{1,0},{2,1},{3,2},{4,3},{5,4},{6,5},{7,6},{9,8},{10,9},{11,10},{12... | collective-permute-start | bytes 393224 | tf_op jit(solution)/shard_map/while/body/eval_jaxpr/ppermute | solution.py:25
  83.0 2.4 %collective-permute-start.1 = (f32[1,128,256]{1,2,0:T(8,128)S(1)}, f32[1,128,256]{1,2,0:T(8,128)S(1)}, u32[]{:S(2)}, u32[]{:S(2)}) collective-permute-start(f32[1,128,256]{1,2,0:T(8,128)S(1)} %get-tuple-element.78), channel_id=1, source_target_pairs={{0,1},{1,2},{2,3},{3,4},{4,5},{5,6},{6,7},{8,9},{9,10},{10,11},{11... | collective-permute-start | bytes 393224 | tf_op jit(solution)/shard_map/while/body/eval_jaxpr/ppermute | solution.py:22
  85.5 3.8 %collective-permute-done.1 = f32[1,128,256]{1,2,0:T(8,128)S(1)} collective-permute-done((f32[1,128,256]{1,2,0:T(8,128)S(1)}, f32[1,128,256]{1,2,0:T(8,128)S(1)}, u32[]{:S(2)}, u32[]{:S(2)}) %collective-permute-start.1) | collective-permute-done | bytes 131104 | tf_op jit(solution)/shard_map/while/body/eval_jaxpr/ppermute | solution.py:22
  91.2 1.9 %collective-permute-start = (f32[1,128,256]{1,2,0:T(8,128)S(1)}, f32[1,128,256]{1,2,0:T(8,128)S(1)}, u32[]{:S(2)}, u32[]{:S(2)}) collective-permute-start(f32[1,128,256]{1,2,0:T(8,128)S(1)} %get-tuple-element.77), channel_id=1, source_target_pairs={{1,0},{2,1},{3,2},{4,3},{5,4},{6,5},{7,6},{9,8},{10,9},{11,10},{12... | collective-permute-start | bytes 393224 | tf_op jit(solution)/shard_map/while/body/eval_jaxpr/ppermute | solution.py:25
  93.2 2.4 %collective-permute-start.1 = (f32[1,128,256]{1,2,0:T(8,128)S(1)}, f32[1,128,256]{1,2,0:T(8,128)S(1)}, u32[]{:S(2)}, u32[]{:S(2)}) collective-permute-start(f32[1,128,256]{1,2,0:T(8,128)S(1)} %get-tuple-element.78), channel_id=1, source_target_pairs={{0,1},{1,2},{2,3},{3,4},{4,5},{5,6},{6,7},{8,9},{9,10},{10,11},{11... | collective-permute-start | bytes 393224 | tf_op jit(solution)/shard_map/while/body/eval_jaxpr/ppermute | solution.py:22
  95.7 3.8 %collective-permute-done.1 = f32[1,128,256]{1,2,0:T(8,128)S(1)} collective-permute-done((f32[1,128,256]{1,2,0:T(8,128)S(1)}, f32[1,128,256]{1,2,0:T(8,128)S(1)}, u32[]{:S(2)}, u32[]{:S(2)}) %collective-permute-start.1) | collective-permute-done | bytes 131104 | tf_op jit(solution)/shard_map/while/body/eval_jaxpr/ppermute | solution.py:22
  99.5 1.9 %convolution_bitcast_fusion.2 = f32[3,128,256]{1,2,0:T(8,128)S(1)} fusion(f32[4,3,256,256]{2,3,1,0:T(8,128)} %get-tuple-element.94, s32[]{:T(128)S(6)} %copy.42, f32[128,256]{0,1:T(8,128)S(1)} %get-tuple-element.87), kind=kOutput, calls=%fused_computation.clone.1 | convolution fusion | flops 301989888 | bytes 1310724 | tf_op jit(solution)/shard_map/while/body/eval_jaxpr/rw,swu->sru/dot_general | solution.py:49
  101.4 1.9 %collective-permute-start = (f32[1,128,256]{1,2,0:T(8,128)S(1)}, f32[1,128,256]{1,2,0:T(8,128)S(1)}, u32[]{:S(2)}, u32[]{:S(2)}) collective-permute-start(f32[1,128,256]{1,2,0:T(8,128)S(1)} %get-tuple-element.77), channel_id=1, source_target_pairs={{1,0},{2,1},{3,2},{4,3},{5,4},{6,5},{7,6},{9,8},{10,9},{11,10},{12... | collective-permute-start | bytes 393224 | tf_op jit(solution)/shard_map/while/body/eval_jaxpr/ppermute | solution.py:25
  103.4 2.4 %collective-permute-start.1 = (f32[1,128,256]{1,2,0:T(8,128)S(1)}, f32[1,128,256]{1,2,0:T(8,128)S(1)}, u32[]{:S(2)}, u32[]{:S(2)}) collective-permute-start(f32[1,128,256]{1,2,0:T(8,128)S(1)} %get-tuple-element.78), channel_id=1, source_target_pairs={{0,1},{1,2},{2,3},{3,4},{4,5},{5,6},{6,7},{8,9},{9,10},{10,11},{11... | collective-permute-start | bytes 393224 | tf_op jit(solution)/shard_map/while/body/eval_jaxpr/ppermute | solution.py:22
  105.9 3.8 %collective-permute-done.1 = f32[1,128,256]{1,2,0:T(8,128)S(1)} collective-permute-done((f32[1,128,256]{1,2,0:T(8,128)S(1)}, f32[1,128,256]{1,2,0:T(8,128)S(1)}, u32[]{:S(2)}, u32[]{:S(2)}) %collective-permute-start.1) | collective-permute-done | bytes 131104 | tf_op jit(solution)/shard_map/while/body/eval_jaxpr/ppermute | solution.py:22
  111.7 1.9 %collective-permute-start = (f32[1,128,256]{1,2,0:T(8,128)S(1)}, f32[1,128,256]{1,2,0:T(8,128)S(1)}, u32[]{:S(2)}, u32[]{:S(2)}) collective-permute-start(f32[1,128,256]{1,2,0:T(8,128)S(1)} %get-tuple-element.77), channel_id=1, source_target_pairs={{1,0},{2,1},{3,2},{4,3},{5,4},{6,5},{7,6},{9,8},{10,9},{11,10},{12... | collective-permute-start | bytes 393224 | tf_op jit(solution)/shard_map/while/body/eval_jaxpr/ppermute | solution.py:25
  113.6 2.4 %collective-permute-start.1 = (f32[1,128,256]{1,2,0:T(8,128)S(1)}, f32[1,128,256]{1,2,0:T(8,128)S(1)}, u32[]{:S(2)}, u32[]{:S(2)}) collective-permute-start(f32[1,128,256]{1,2,0:T(8,128)S(1)} %get-tuple-element.78), channel_id=1, source_target_pairs={{0,1},{1,2},{2,3},{3,4},{4,5},{5,6},{6,7},{8,9},{9,10},{10,11},{11... | collective-permute-start | bytes 393224 | tf_op jit(solution)/shard_map/while/body/eval_jaxpr/ppermute | solution.py:22
  116.1 3.8 %collective-permute-done.1 = f32[1,128,256]{1,2,0:T(8,128)S(1)} collective-permute-done((f32[1,128,256]{1,2,0:T(8,128)S(1)}, f32[1,128,256]{1,2,0:T(8,128)S(1)}, u32[]{:S(2)}, u32[]{:S(2)}) %collective-permute-start.1) | collective-permute-done | bytes 131104 | tf_op jit(solution)/shard_map/while/body/eval_jaxpr/ppermute | solution.py:22
  119.9 10.6 %all_to_all.12 = f32[4,128,256]{1,2,0:T(8,128)S(1)} all-to-all(f32[4,128,256]{1,2,0:T(8,128)S(1)} %get-tuple-element.27), channel_id=1, replica_groups=mesh['site'=4,'sector'=8] {'site'}, dimensions={0} | all-to-all | bytes 1048576 | tf_op jit(solution)/shard_map/all_to_all | solution.py:56
  (48 shorter events, 20.1 us)
Async XLA Ops:
  0.0 3.0 %copy-start = (bf16[1,256,8,256]{3,2,1,0:T(8,128)(2,1)S(1)}, bf16[1,256,8,256]{3,2,1,0:T(8,128)(2,1)}, u32[]{:S(2)}) copy-start(bf16[1,256,8,256]{3,2,1,0:T(8,128)(2,1)} %param.9) | copy-start | bytes 3145732
  0.0 6.7 %copy-start.5 = (s32[1,8]{1,0:T(1,128)S(1)}, s32[1,8]{1,0:T(1,128)}, u32[]{:S(2)}) copy-start(s32[1,8]{1,0:T(1,128)} %param.10) | copy-start | bytes 100
  9.7 20.2 %collective-permute-start.2 = (f32[1,3,256,256]{3,2,1,0:T(8,128)S(1)}, f32[1,3,256,256]{3,2,1,0:T(8,128)S(1)}, u32[]{:S(2)}, u32[]{:S(2)}) collective-permute-start(f32[1,3,256,256]{3,2,1,0:T(8,128)S(1)} %copy.12), channel_id=1, source_target_pairs={{0,8},{8,16},{16,24},{24,0},{1,9},{9,17},{17,25},{25,1},{2,10},{10... | collective-permute-start | bytes 2359304 | tf_op jit(solution)/shard_map/ppermute | solution.py:11
  30.0 0.9 copy-start.3
  30.9 19.4 %collective-permute-start.3 = (f32[1,3,256,256]{3,2,1,0:T(8,128)S(1)}, f32[1,3,256,256]{3,2,1,0:T(8,128)}, u32[]{:S(2)}, u32[]{:S(2)}) collective-permute-start(f32[1,3,256,256]{3,2,1,0:T(8,128)S(1)} %collective-permute-done.2), channel_id=1, source_target_pairs={{0,8},{8,16},{16,24},{24,0},{1,9},{9,17},{17,25},{25,1},{2,10},{10... | collective-permute-start | bytes 2359304 | tf_op jit(solution)/shard_map/ppermute | solution.py:11
  50.3 18.8 %collective-permute-start.4 = (f32[1,3,256,256]{3,2,1,0:T(8,128)}, f32[1,3,256,256]{3,2,1,0:T(8,128)}, u32[]{:S(2)}, u32[]{:S(2)}) collective-permute-start(f32[1,3,256,256]{3,2,1,0:T(8,128)} %collective-permute-done.3), channel_id=1, source_target_pairs={{0,8},{8,16},{16,24},{24,0},{1,9},{9,17},{17,25},{25,1},{2,10},{10... | collective-permute-start | bytes 2359304 | tf_op jit(solution)/shard_map/ppermute | solution.py:11
  71.5 3.6 %copy-start.2 = (f32[1,3,256,256]{2,1,3,0:T(4,128)S(1)}, f32[1,3,256,256]{2,1,3,0:T(4,128)}, u32[]{:S(2)}) copy-start(f32[1,3,256,256]{2,1,3,0:T(4,128)} %copy.13) | copy-start | bytes 2359300
  71.5 3.8 %copy-start.1 = (f32[1,3,256,256]{2,1,3,0:T(4,128)S(1)}, f32[1,3,256,256]{2,1,3,0:T(4,128)}, u32[]{:S(2)}) copy-start(f32[1,3,256,256]{2,1,3,0:T(4,128)} %copy.14) | copy-start | bytes 2359300
  76.1 2.9 %copy-start.4 = (f32[4,128,256]{1,2,0:T(8,128)S(1)}, f32[4,128,256]{1,2,0:T(8,128)}, u32[]{:S(2)}) copy-start(f32[4,128,256]{1,2,0:T(8,128)} %custom-call.1) | copy-start | bytes 1572868
  81.0 4.4 %collective-permute-start = (f32[1,128,256]{1,2,0:T(8,128)S(1)}, f32[1,128,256]{1,2,0:T(8,128)S(1)}, u32[]{:S(2)}, u32[]{:S(2)}) collective-permute-start(f32[1,128,256]{1,2,0:T(8,128)S(1)} %get-tuple-element.77), channel_id=1, source_target_pairs={{1,0},{2,1},{3,2},{4,3},{5,4},{6,5},{7,6},{9,8},{10,9},{11,10},{12... | collective-permute-start | bytes 393224 | tf_op jit(solution)/shard_map/while/body/eval_jaxpr/ppermute | solution.py:25
  83.0 6.3 %collective-permute-start.1 = (f32[1,128,256]{1,2,0:T(8,128)S(1)}, f32[1,128,256]{1,2,0:T(8,128)S(1)}, u32[]{:S(2)}, u32[]{:S(2)}) collective-permute-start(f32[1,128,256]{1,2,0:T(8,128)S(1)} %get-tuple-element.78), channel_id=1, source_target_pairs={{0,1},{1,2},{2,3},{3,4},{4,5},{5,6},{6,7},{8,9},{9,10},{10,11},{11... | collective-permute-start | bytes 393224 | tf_op jit(solution)/shard_map/while/body/eval_jaxpr/ppermute | solution.py:22
  91.2 4.4 %collective-permute-start = (f32[1,128,256]{1,2,0:T(8,128)S(1)}, f32[1,128,256]{1,2,0:T(8,128)S(1)}, u32[]{:S(2)}, u32[]{:S(2)}) collective-permute-start(f32[1,128,256]{1,2,0:T(8,128)S(1)} %get-tuple-element.77), channel_id=1, source_target_pairs={{1,0},{2,1},{3,2},{4,3},{5,4},{6,5},{7,6},{9,8},{10,9},{11,10},{12... | collective-permute-start | bytes 393224 | tf_op jit(solution)/shard_map/while/body/eval_jaxpr/ppermute | solution.py:25
  93.2 6.3 %collective-permute-start.1 = (f32[1,128,256]{1,2,0:T(8,128)S(1)}, f32[1,128,256]{1,2,0:T(8,128)S(1)}, u32[]{:S(2)}, u32[]{:S(2)}) collective-permute-start(f32[1,128,256]{1,2,0:T(8,128)S(1)} %get-tuple-element.78), channel_id=1, source_target_pairs={{0,1},{1,2},{2,3},{3,4},{4,5},{5,6},{6,7},{8,9},{9,10},{10,11},{11... | collective-permute-start | bytes 393224 | tf_op jit(solution)/shard_map/while/body/eval_jaxpr/ppermute | solution.py:22
  101.4 4.4 %collective-permute-start = (f32[1,128,256]{1,2,0:T(8,128)S(1)}, f32[1,128,256]{1,2,0:T(8,128)S(1)}, u32[]{:S(2)}, u32[]{:S(2)}) collective-permute-start(f32[1,128,256]{1,2,0:T(8,128)S(1)} %get-tuple-element.77), channel_id=1, source_target_pairs={{1,0},{2,1},{3,2},{4,3},{5,4},{6,5},{7,6},{9,8},{10,9},{11,10},{12... | collective-permute-start | bytes 393224 | tf_op jit(solution)/shard_map/while/body/eval_jaxpr/ppermute | solution.py:25
  103.4 6.3 %collective-permute-start.1 = (f32[1,128,256]{1,2,0:T(8,128)S(1)}, f32[1,128,256]{1,2,0:T(8,128)S(1)}, u32[]{:S(2)}, u32[]{:S(2)}) collective-permute-start(f32[1,128,256]{1,2,0:T(8,128)S(1)} %get-tuple-element.78), channel_id=1, source_target_pairs={{0,1},{1,2},{2,3},{3,4},{4,5},{5,6},{6,7},{8,9},{9,10},{10,11},{11... | collective-permute-start | bytes 393224 | tf_op jit(solution)/shard_map/while/body/eval_jaxpr/ppermute | solution.py:22
  111.7 4.4 %collective-permute-start = (f32[1,128,256]{1,2,0:T(8,128)S(1)}, f32[1,128,256]{1,2,0:T(8,128)S(1)}, u32[]{:S(2)}, u32[]{:S(2)}) collective-permute-start(f32[1,128,256]{1,2,0:T(8,128)S(1)} %get-tuple-element.77), channel_id=1, source_target_pairs={{1,0},{2,1},{3,2},{4,3},{5,4},{6,5},{7,6},{9,8},{10,9},{11,10},{12... | collective-permute-start | bytes 393224 | tf_op jit(solution)/shard_map/while/body/eval_jaxpr/ppermute | solution.py:25
  113.6 6.3 %collective-permute-start.1 = (f32[1,128,256]{1,2,0:T(8,128)S(1)}, f32[1,128,256]{1,2,0:T(8,128)S(1)}, u32[]{:S(2)}, u32[]{:S(2)}) collective-permute-start(f32[1,128,256]{1,2,0:T(8,128)S(1)} %get-tuple-element.78), channel_id=1, source_target_pairs={{0,1},{1,2},{2,3},{3,4},{4,5},{5,6},{6,7},{8,9},{9,10},{10,11},{11... | collective-permute-start | bytes 393224 | tf_op jit(solution)/shard_map/while/body/eval_jaxpr/ppermute | solution.py:22
